TPU v7x, 32 devices: a whole 2x2x4 slice. The times are simulated.
32 devices in a mesh: row: 4 (over y, x), col: 8 (over z, core).
Axes of the slice: x: 2, y: 2, z: 4, core: 2. Of those that a mesh axis runs over, the one named last changes fastest.
Arguments:
- vectors: float32 [32, 32768], P(None, ('row', 'col'))
- tiles: float32 [4096, 128, 128], P(('row', 'col'))
- tile_row: int32 [32, 128], P(('row', 'col')), may hold values from 0 to 63, never falling along the last dimension, each value on 1 to 6 neighbouring positions
- tile_col: int32 [32, 128], P(('row', 'col')), may hold values from 0 to 31
Outputs:
- filtered: float32 [32, 32768], P(None, ('row', 'col'))
- gram: float32 [32, 32], replicated
Inputs may be any that keep to these rules, and one draw needn't show every extreme that they name: `tile_row`: on each device the entries never fall along the last dimension, and each of the 64 values is taken by 1 to 6 slots.
All inputs are finite; a program needn't handle non-finite values.
Results may differ from a plain program's by a relative error of at most 0.00015.
Values sent between devices are 32-bit elements; how exact they have to be, the bound alone decides.
No kernel may reach another device: no remote copies, remote signals or barrier semaphores. Data moves between devices by JAX's collectives and lax.ppermute only.
A program may use at most 64 MiB of HBM per device.

v0:
```python
import jax
import jax.numpy as jnp
from jax import lax
from jax.sharding import PartitionSpec as P

TB = 128
K = 32
STEPS = 3


def on_device(vectors, tiles, tile_row, tile_col):
    rows_here = tile_row[0]
    cols_here = tile_col[0]
    n_row = lax.axis_size("row")
    n_col = lax.axis_size("col")
    width = vectors.shape[1]
    owned = width // TB
    local_rows = n_col * owned
    local_cols = n_row * owned
    onehot = (rows_here[:, None] == jnp.arange(local_rows, dtype=jnp.int32)[None, :]).astype(
        jnp.float32
    )
    magnitude = jnp.sum(jnp.abs(tiles), axis=2)
    row_terms = jnp.einsum("ti,tl->li", magnitude, onehot, precision=lax.Precision.HIGHEST).reshape(
        local_rows * TB
    )
    degree = 1.0 + lax.psum_scatter(row_terms, "col", scatter_dimension=0, tiled=True)
    scale = 1.0 / jnp.sqrt(degree)

    def operate(current):
        scaled = current * scale[None, :]
        panel = lax.all_gather(scaled, "row", axis=1, tiled=True)
        picked = jnp.take(panel.reshape(K, local_cols, TB), cols_here, axis=1)
        product = jnp.einsum("tij,ktj->kti", tiles, picked, precision=lax.Precision.HIGHEST)
        partial_value = jnp.einsum(
            "kti,tl->kli", product, onehot, precision=lax.Precision.HIGHEST
        ).reshape(K, local_rows * TB)
        mine = lax.psum_scatter(partial_value, "col", scatter_dimension=1, tiled=True)
        return mine * scale[None, :]

    previous = vectors
    current = operate(vectors)
    for step in range(STEPS - 1):
        following = 2.0 * operate(current) - previous
        previous = current
        current = following
    local_gram = jnp.dot(current, current.T, precision=lax.Precision.HIGHEST)
    gram = lax.psum(local_gram, ("row", "col")) / (width * n_row * n_col)
    return (current, gram)


def solution(mesh):
    in_specs = (
        P(None, ("row", "col")),
        P(("row", "col"), None, None),
        P(("row", "col"), None),
        P(("row", "col"), None),
    )
    out_specs = (P(None, ("row", "col")), P())
    return jax.shard_map(
        on_device, mesh=mesh, in_specs=in_specs, out_specs=out_specs, check_vma=False
    )
```

profile of v0, /device:TPU:10, one launch (start us, length us, event | category | flops | bytes accessed | tf_op | source)
XLA Modules:
  0.0 275.3 jit_solution(16175437541620134693)
XLA Ops:
  7.2 0.0 reduce-scatter.4.cloned.1.call-start
  7.2 0.7 compare_and_fusion
  7.9 0.7 compare_select_fusion
  8.6 0.0 copy-start.4
  8.6 0.0 copy-start.1
  8.6 5.7 %abs_reduce_fusion = f32[128,128]{1,0:T(8,128)S(1)} fusion(f32[128,128,128]{2,1,0:T(8,128)} %param.7), kind=kLoop, calls=%fused_computation.3 | loop fusion | flops 4177920 | bytes 8454144 | tf_op jit(solution)/shard_map/reduce_sum | solution.py:23
  14.2 0.0 copy-done.3
  14.2 0.2 convolution_bitcast_fusion
  14.4 25.2 %all-reduce = f32[8192]{0:T(1024)S(1)} all-reduce(f32[8192]{0:T(1024)S(1)} %convolution_bitcast_fusion), channel_id=2, replica_groups=mesh['row'=4,'col'=8] {'col'}, use_global_device_ids=true, to_apply=%region_1.0.clone | all-reduce | flops 8192 | bytes 65536
  39.6 0.0 copy-done.4
  39.6 0.6 dynamic-slice
  40.9 0.0 copy-done.1
  40.9 10.1 %all_gather.9 = f32[32,4096]{1,0:T(8,128)S(1)} all-gather(f32[32,1024]{1,0:T(8,128)S(1)} %broadcast_multiply_fusion), channel_id=1, replica_groups=mesh['row'=4,'col'=8] {'row'}, dimensions={1}, use_global_device_ids=true | all-gather | bytes 655360 | tf_op jit(solution)/shard_map/all_gather | solution.py:32
  51.0 0.1 copy_bitcast_fusion.5
  51.0 0.8 gather_fusion
  51.8 15.5 %fusion.15 = f32[32,128,128]{2,0,1:T(8,128)S(1)} fusion(f32[128,128,128]{2,1,0:T(8,128)} %param.7, f32[128,32,128]{2,1,0:T(8,128)S(1)} %gather_fusion, pred[128]{0:T(512)(128)(4,1)S(1)} %compare_and_fusion), kind=kOutput, calls=%fused_computation.19 | convolution fusion | flops 805830656 | bytes 12583040 | tf_op jit(solution)/shard_map/tij,ktj->kti/dot_general | solution.py:34
  67.3 2.1 fusion.10
  69.4 1.6 copy.38
  71.0 0.0 reduce-scatter.4.cloned.1.call-update
  71.0 0.0 reduce-scatter.6.cloned.1.call-start
  71.1 29.3 %reduce-scatter.4.cloned.1.call-done = f32[32,1024]{1,0:T(8,128)} async-done(((f32[32,8192]{1,0:T(8,128)}), f32[32,1024]{1,0:T(8,128)}) %reduce-scatter.4.cloned.1.call-update) | async-done | bytes 131088 | tf_op jit(solution)/shard_map/reduce_scatter | solution.py:38
  100.4 0.9 multiply_multiply_fusion
  101.3 10.5 %all_gather.10 = f32[32,4096]{1,0:T(8,128)S(1)} all-gather(f32[32,1024]{1,0:T(8,128)S(1)} %multiply_multiply_fusion), channel_id=1, replica_groups=mesh['row'=4,'col'=8] {'row'}, dimensions={1}, use_global_device_ids=true | all-gather | bytes 655360 | tf_op jit(solution)/shard_map/all_gather | solution.py:32
  111.8 0.1 copy_bitcast_fusion.4
  111.8 0.8 gather_fusion.1
  112.6 15.5 %fusion.18 = f32[32,128,128]{2,0,1:T(8,128)S(1)} fusion(f32[128,128,128]{2,1,0:T(8,128)} %param.7, f32[128,32,128]{2,1,0:T(8,128)S(1)} %gather_fusion.1, pred[128]{0:T(512)(128)(4,1)S(1)} %compare_and_fusion), kind=kOutput, calls=%fused_computation.20 | convolution fusion | flops 805830656 | bytes 12583040 | tf_op jit(solution)/shard_map/tij,ktj->kti/dot_general | solution.py:34
  128.1 2.1 fusion.8
  130.2 1.6 copy.37
  131.8 0.0 reduce-scatter.6.cloned.1.call-update
  131.8 0.0 reduce-scatter.8.cloned.1.call-start
  131.9 30.1 %reduce-scatter.6.cloned.1.call-done = f32[32,1024]{1,0:T(8,128)} async-done(((f32[32,8192]{1,0:T(8,128)}), f32[32,1024]{1,0:T(8,128)}) %reduce-scatter.6.cloned.1.call-update) | async-done | bytes 131088 | tf_op jit(solution)/shard_map/reduce_scatter | solution.py:38
  162.0 0.9 subtract_multiply_fusion
  162.9 9.8 %all_gather.11 = f32[32,4096]{1,0:T(8,128)S(1)} all-gather(f32[32,1024]{1,0:T(8,128)S(1)} %subtract_multiply_fusion), channel_id=1, replica_groups=mesh['row'=4,'col'=8] {'row'}, dimensions={1}, use_global_device_ids=true | all-gather | bytes 655360 | tf_op jit(solution)/shard_map/all_gather | solution.py:32
  172.7 0.1 copy_bitcast_fusion.3
  172.8 0.8 gather_fusion.2
  173.6 15.5 %fusion.21 = f32[32,128,128]{2,0,1:T(8,128)S(1)} fusion(f32[128,128,128]{2,1,0:T(8,128)} %param.7, f32[128,32,128]{2,1,0:T(8,128)S(1)} %gather_fusion.2, pred[128]{0:T(512)(128)(4,1)S(1)} %compare_and_fusion), kind=kOutput, calls=%fused_computation.21 | convolution fusion | flops 805830656 | bytes 12583040 | tf_op jit(solution)/shard_map/tij,ktj->kti/dot_general | solution.py:34
  189.1 2.1 fusion.6
  191.2 0.0 copy-start.2
  191.2 1.6 copy.36
  192.8 0.0 reduce-scatter.8.cloned.1.call-update
  192.8 30.6 %reduce-scatter.8.cloned.1.call-done = f32[32,1024]{1,0:T(8,128)} async-done(((f32[32,8192]{1,0:T(8,128)}), f32[32,1024]{1,0:T(8,128)}) %reduce-scatter.8.cloned.1.call-update) | async-done | bytes 131088 | tf_op jit(solution)/shard_map/reduce_scatter | solution.py:38
  223.4 0.0 copy-done.2
  223.4 0.9 multiply_subtract_fusion
  224.3 0.0 copy-start
  224.3 0.3 fusion.42
  224.6 43.5 %psum.7 = f32[32,32]{1,0:T(8,128)S(1)} all-reduce(f32[32,32]{1,0:T(8,128)S(1)} %fusion.42), channel_id=1, replica_groups=mesh['row'=4,'col'=8] {'row','col'}, use_global_device_ids=true, to_apply=%region_5.7 | all-reduce | flops 1024 | bytes 8192 | tf_op jit(solution)/shard_map/psum | solution.py:48
  268.1 0.6 broadcast_multiply_fusion.1
  268.7 0.0 copy-done
  (4 shorter events, 0.0 us)
Async XLA Ops:
  7.2 93.2 %reduce-scatter.4.cloned.1.call-start = ((), (), s32[]{:S(2)}) async-start(), calls=%async_computation.3 | async-start | bytes 1179648 | tf_op jit(solution)/shard_map/reduce_scatter | solution.py:38
  8.5 5.7 %copy-start.3 = (s32[1,128]{1,0:T(1,128)S(1)}, s32[1,128]{1,0:T(1,128)}, u32[]{:S(2)}) copy-start(s32[1,128]{1,0:T(1,128)} %param.8) | copy-start | bytes 1540
  8.6 31.1 %copy-start.4 = (u32[32]{0:T(128)S(1)}, u32[32]{0:T(128)}, u32[]{:S(2)}) copy-start(u32[32]{0:T(128)} %constant.23) | copy-start | bytes 388
  8.6 32.3 %copy-start.1 = (f32[32,1024]{1,0:T(8,128)S(1)}, f32[32,1024]{1,0:T(8,128)}, u32[]{:S(2)}) copy-start(f32[32,1024]{1,0:T(8,128)} %param.6) | copy-start | bytes 393220
  71.0 91.0 %reduce-scatter.6.cloned.1.call-start = ((), (), s32[]{:S(2)}) async-start(), calls=%async_computation.4 | async-start | bytes 1179648 | tf_op jit(solution)/shard_map/reduce_scatter | solution.py:38
  131.8 91.6 %reduce-scatter.8.cloned.1.call-start = ((), (), s32[]{:S(2)}) async-start(), calls=%async_computation.5 | async-start | bytes 1179648 | tf_op jit(solution)/shard_map/reduce_scatter | solution.py:38
  191.2 32.2 %copy-start.2 = (f32[32,1024]{1,0:T(8,128)S(1)}, f32[32,1024]{1,0:T(8,128)}, u32[]{:S(2)}) copy-start(f32[32,1024]{1,0:T(8,128)} %reduce-scatter.4.cloned.1.call-done) | copy-start | bytes 393220
  224.3 44.4 %copy-start = (f32[32,1024]{1,0:T(8,128)}, f32[32,1024]{1,0:T(8,128)S(1)}, u32[]{:S(2)}) copy-start(f32[32,1024]{1,0:T(8,128)S(1)} %multiply_subtract_fusion) | copy-start | bytes 393220
Sparse Core Ops, SparseCore 0:
  71.2 29.1 reduce-scatter.3
  132.0 30.0 reduce-scatter.5
  192.9 30.4 reduce-scatter.7
where the time goes:
time: 276 us; the launch traced here: 275 us
  blocking collectives  99 us (36%)
  waiting for transfers between devices  90.1 us (33%)
  matrix products  53.1 us (19%)
  between operations  14.6 us (5%)
  other arithmetic  10.4 us (4%)
  local copies, waits for them, and re-layouts  7.97 us (3%)
    reduce_scatter x3, waiting for transfers between devices, operate(): lax.psum_scatter(partial_value, 'col', scatter_dimension=1, tiled=True)  90 us
    dot_general x3, matrix products, operate(): jnp.einsum('tij,ktj->kti', tiles, picked, precision=lax.Precision.HIGHEST)  46.4 us
    psum x1, blocking collectives, on_device(): gram = lax.psum(local_gram, ('row', 'col')) / (width * n_row * n_col)  43.5 us
    all_gather x3, blocking collectives, operate(): panel = lax.all_gather(scaled, 'row', axis=1, tiled=True)  30.3 us
    unnamed x1, blocking collectives  25.2 us
    dot_general x3, matrix products, operate(): jnp.einsum('kti,tl->kli', product, onehot, precision=lax.Precision.HIGHEST)  6.25 us
    reduce_sum x1, other arithmetic, on_device(): magnitude = jnp.sum(jnp.abs(tiles), axis=2)  5.65 us
  transfers between devices with their start and end apart: 3, of which 3 were waited for; matrix products, arithmetic and copies ran while one was open for 0% of the time, Pallas kernels for 0%

commit v1 on v0

--- a/solution.py
+++ b/solution.py
@@ -2,10 +2,24 @@
 import jax.numpy as jnp
 from jax import lax
 from jax.sharding import PartitionSpec as P
+from jax.lax import axis_index, ppermute, psum
 
 TB = 128
 K = 32
 STEPS = 3
+
+
+def drive_axis_part(xs, d0=1):
+    value_now, parts_out, all_rows = (psum(1, axis_name="row"), axis_index("row"), xs.shape[d0])
+    block_list = list(map(lambda i0: (i0, (i0 + 1) % value_now), range(value_now)))
+    p_next = jnp.zeros((*xs.shape[:d0], value_now * all_rows, *xs.shape[d0 + 1 :]), xs.dtype)
+    small = xs
+    for jj in tuple(range(value_now)):
+        block_next = (parts_out - jj) % value_now
+        p_next = lax.dynamic_update_slice_in_dim(p_next, small, block_next * all_rows, axis=d0)
+        if jj < value_now - 1:
+            small = ppermute(small, "row", block_list)
+    return p_next
 
 
 def on_device(vectors, tiles, tile_row, tile_col):
@@ -29,7 +43,7 @@
 
     def operate(current):
         scaled = current * scale[None, :]
-        panel = lax.all_gather(scaled, "row", axis=1, tiled=True)
+        panel = drive_axis_part(scaled)
         picked = jnp.take(panel.reshape(K, local_cols, TB), cols_here, axis=1)
         product = jnp.einsum("tij,ktj->kti", tiles, picked, precision=lax.Precision.HIGHEST)
         partial_value = jnp.einsum(

time: 276 us -> 301 us (1.091)
  waiting for transfers between devices: 90.1 us -> 127 us
  blocking collectives: 99 us -> 69.3 us
  starting transfers between devices: 0.12 us -> 20.4 us
    ppermute x0 -> x9, waiting for transfers between devices: none -> 31.6 us  [drive_axis_part(): small = ppermute(small, 'row', block_list)]
    all_gather x3 -> x0, blocking collectives: 30.3 us -> none  [operate(): panel = lax.all_gather(scaled, 'row', axis=1, tiled=True)]
    ppermute x0 -> x9, starting transfers between devices: none -> 20.2 us  [drive_axis_part(): small = ppermute(small, 'row', block_list)]
    reduce_scatter x3, waiting for transfers between devices: 90 us -> 94.9 us  [operate(): lax.psum_scatter(partial_value, 'col', scatter_dimension=1, tiled=True)]
  transfers between devices with their start and end apart: 3 -> 12, of which waited for: 3 -> 12; matrix products, arithmetic and copies ran while one was open for 0% -> 0% of each run, Pallas kernels for 0% -> 0%
where the time goes in v1:
time: 301 us
  waiting for transfers between devices  127 us (42%)
  blocking collectives  69.3 us (23%)
  matrix products  53.1 us (18%)
  starting transfers between devices  20.4 us (7%)
  between operations  14.7 us (5%)
  other arithmetic  9.11 us (3%)
  local copies, waits for them, and re-layouts  8.11 us (3%)
    reduce_scatter x3, waiting for transfers between devices, operate(): lax.psum_scatter(partial_value, 'col', scatter_dimension=1, tiled=True)  94.9 us
    dot_general x3, matrix products, operate(): jnp.einsum('tij,ktj->kti', tiles, picked, precision=lax.Precision.HIGHEST)  46.4 us
    psum x1, blocking collectives, on_device(): gram = lax.psum(local_gram, ('row', 'col')) / (width * n_row * n_col)  44 us
    ppermute x9, waiting for transfers between devices, drive_axis_part(): small = ppermute(small, 'row', block_list)  31.6 us
    unnamed x1, blocking collectives  25.2 us
    ppermute x9, starting transfers between devices, drive_axis_part(): small = ppermute(small, 'row', block_list)  20.2 us
    dot_general x3, matrix products, operate(): jnp.einsum('kti,tl->kli', product, onehot, precision=lax.Precision.HIGHEST)  6.24 us
  transfers between devices with their start and end apart: 12, of which 12 were waited for; matrix products, arithmetic and copies ran while one was open for 0% of the time, Pallas kernels for 0%

profile of v1, /device:TPU:10, one launch (start us, length us, event | category | flops | bytes accessed | tf_op | source)
XLA Modules:
  0.0 301.2 jit_solution(17734130623007926917)
XLA Ops:
  7.3 5.7 %abs_reduce_fusion = f32[128,128]{1,0:T(8,128)S(1)} fusion(f32[128,128,128]{2,1,0:T(8,128)} %param.7), kind=kLoop, calls=%fused_computation.3 | loop fusion | flops 4177920 | bytes 8454144 | tf_op jit(solution)/shard_map/reduce_sum | solution.py:37
  13.0 0.2 convolution_bitcast_fusion
  13.1 25.2 %all-reduce = f32[8192]{0:T(1024)S(1)} all-reduce(f32[8192]{0:T(1024)S(1)} %convolution_bitcast_fusion), channel_id=2, replica_groups=mesh['row'=4,'col'=8] {'col'}, use_global_device_ids=true, to_apply=%region_1.0.clone | all-reduce | flops 8192 | bytes 65536
  38.3 0.6 dynamic-slice
  39.7 1.5 collective-permute-start
  41.2 4.1 %collective-permute-done = f32[32,1024]{1,0:T(8,128)S(1)} collective-permute-done((f32[32,1024]{1,0:T(8,128)S(1)}, f32[32,1024]{1,0:T(8,128)S(1)}, u32[]{:S(2)}, u32[]{:S(2)}) %collective-permute-start) | collective-permute-done | bytes 131104 | tf_op jit(solution)/shard_map/ppermute | solution.py:21
  45.3 3.0 %collective-permute-start.1 = (f32[32,1024]{1,0:T(8,128)S(1)}, f32[32,1024]{1,0:T(8,128)S(1)}, u32[]{:S(2)}, u32[]{:S(2)}) collective-permute-start(f32[32,1024]{1,0:T(8,128)S(1)} %collective-permute-done), channel_id=1, source_target_pairs={{0,8},{8,16},{16,24},{24,0},{1,9},{9,17},{17,25},{25,1},{2,10},{10... | collective-permute-start | bytes 393224 | tf_op jit(solution)/shard_map/ppermute | solution.py:21
  48.4 3.0 %collective-permute-done.1 = f32[32,1024]{1,0:T(8,128)S(1)} collective-permute-done((f32[32,1024]{1,0:T(8,128)S(1)}, f32[32,1024]{1,0:T(8,128)S(1)}, u32[]{:S(2)}, u32[]{:S(2)}) %collective-permute-start.1) | collective-permute-done | bytes 131104 | tf_op jit(solution)/shard_map/ppermute | solution.py:21
  51.4 3.4 %collective-permute-start.2 = (f32[32,1024]{1,0:T(8,128)S(1)}, f32[32,1024]{1,0:T(8,128)S(1)}, u32[]{:S(2)}, u32[]{:S(2)}) collective-permute-start(f32[32,1024]{1,0:T(8,128)S(1)} %collective-permute-done.1), channel_id=1, source_target_pairs={{0,8},{8,16},{16,24},{24,0},{1,9},{9,17},{17,25},{25,1},{2,10},{10... | collective-permute-start | bytes 393224 | tf_op jit(solution)/shard_map/ppermute | solution.py:21
  54.8 2.5 collective-permute-done.2
  57.3 0.1 copy_bitcast_fusion.5
  57.4 0.8 gather_fusion
  58.2 15.5 %fusion.15 = f32[32,128,128]{2,0,1:T(8,128)S(1)} fusion(f32[128,128,128]{2,1,0:T(8,128)} %param.7, f32[128,32,128]{2,1,0:T(8,128)S(1)} %gather_fusion, pred[128]{0:T(512)(128)(4,1)S(1)} %compare_and_fusion), kind=kOutput, calls=%fused_computation.19 | convolution fusion | flops 805830656 | bytes 12583040 | tf_op jit(solution)/shard_map/tij,ktj->kti/dot_general | solution.py:48
  73.7 2.1 fusion.10
  75.7 1.6 copy.38
  77.3 0.0 reduce-scatter.6.cloned.1.call-start
  77.4 31.6 %reduce-scatter.4.cloned.1.call-done = f32[32,1024]{1,0:T(8,128)} async-done(((f32[32,8192]{1,0:T(8,128)}), f32[32,1024]{1,0:T(8,128)}) %reduce-scatter.4.cloned.1.call-update) | async-done | bytes 131088 | tf_op jit(solution)/shard_map/reduce_scatter | solution.py:52
  109.0 0.9 constant_dynamic-update-slice_fusion.7
  109.9 1.5 collective-permute-start.3
  111.4 4.7 %collective-permute-done.3 = f32[32,1024]{1,0:T(8,128)S(1)} collective-permute-done((f32[32,1024]{1,0:T(8,128)S(1)}, f32[32,1024]{1,0:T(8,128)S(1)}, u32[]{:S(2)}, u32[]{:S(2)}) %collective-permute-start.3) | collective-permute-done | bytes 131104 | tf_op jit(solution)/shard_map/ppermute | solution.py:21
  116.2 1.8 collective-permute-start.4
  118.0 3.5 %collective-permute-done.4 = f32[32,1024]{1,0:T(8,128)S(1)} collective-permute-done((f32[32,1024]{1,0:T(8,128)S(1)}, f32[32,1024]{1,0:T(8,128)S(1)}, u32[]{:S(2)}, u32[]{:S(2)}) %collective-permute-start.4) | collective-permute-done | bytes 131104 | tf_op jit(solution)/shard_map/ppermute | solution.py:21
  121.5 3.3 %collective-permute-start.5 = (f32[32,1024]{1,0:T(8,128)S(1)}, f32[32,1024]{1,0:T(8,128)S(1)}, u32[]{:S(2)}, u32[]{:S(2)}) collective-permute-start(f32[32,1024]{1,0:T(8,128)S(1)} %collective-permute-done.4), channel_id=1, source_target_pairs={{0,8},{8,16},{16,24},{24,0},{1,9},{9,17},{17,25},{25,1},{2,10},{10... | collective-permute-start | bytes 393224 | tf_op jit(solution)/shard_map/ppermute | solution.py:21
  124.9 2.5 collective-permute-done.5
  127.4 0.1 copy_bitcast_fusion.4
  127.4 0.8 gather_fusion.1
  128.2 15.5 %fusion.18 = f32[32,128,128]{2,0,1:T(8,128)S(1)} fusion(f32[128,128,128]{2,1,0:T(8,128)} %param.7, f32[128,32,128]{2,1,0:T(8,128)S(1)} %gather_fusion.1, pred[128]{0:T(512)(128)(4,1)S(1)} %compare_and_fusion), kind=kOutput, calls=%fused_computation.20 | convolution fusion | flops 805830656 | bytes 12583040 | tf_op jit(solution)/shard_map/tij,ktj->kti/dot_general | solution.py:48
  143.7 2.1 fusion.8
  145.8 1.6 copy.37
  147.4 0.0 reduce-scatter.8.cloned.1.call-start
  147.5 31.7 %reduce-scatter.6.cloned.1.call-done = f32[32,1024]{1,0:T(8,128)} async-done(((f32[32,8192]{1,0:T(8,128)}), f32[32,1024]{1,0:T(8,128)}) %reduce-scatter.6.cloned.1.call-update) | async-done | bytes 131088 | tf_op jit(solution)/shard_map/reduce_scatter | solution.py:52
  179.2 0.9 constant_dynamic-update-slice_fusion.3
  180.2 1.1 collective-permute-start.6
  181.3 4.9 %collective-permute-done.6 = f32[32,1024]{1,0:T(8,128)S(1)} collective-permute-done((f32[32,1024]{1,0:T(8,128)S(1)}, f32[32,1024]{1,0:T(8,128)S(1)}, u32[]{:S(2)}, u32[]{:S(2)}) %collective-permute-start.6) | collective-permute-done | bytes 131104 | tf_op jit(solution)/shard_map/ppermute | solution.py:21
  186.2 1.3 collective-permute-start.7
  187.5 3.9 %collective-permute-done.7 = f32[32,1024]{1,0:T(8,128)S(1)} collective-permute-done((f32[32,1024]{1,0:T(8,128)S(1)}, f32[32,1024]{1,0:T(8,128)S(1)}, u32[]{:S(2)}, u32[]{:S(2)}) %collective-permute-start.7) | collective-permute-done | bytes 131104 | tf_op jit(solution)/shard_map/ppermute | solution.py:21
  191.4 3.3 %collective-permute-start.8 = (f32[32,1024]{1,0:T(8,128)S(1)}, f32[32,1024]{1,0:T(8,128)S(1)}, u32[]{:S(2)}, u32[]{:S(2)}) collective-permute-start(f32[32,1024]{1,0:T(8,128)S(1)} %collective-permute-done.7), channel_id=1, source_target_pairs={{0,8},{8,16},{16,24},{24,0},{1,9},{9,17},{17,25},{25,1},{2,10},{10... | collective-permute-start | bytes 393224 | tf_op jit(solution)/shard_map/ppermute | solution.py:21
  194.7 2.5 collective-permute-done.8
  197.2 0.1 copy_bitcast_fusion.3
  197.2 0.8 gather_fusion.2
  198.0 15.5 %fusion.21 = f32[32,128,128]{2,0,1:T(8,128)S(1)} fusion(f32[128,128,128]{2,1,0:T(8,128)} %param.7, f32[128,32,128]{2,1,0:T(8,128)S(1)} %gather_fusion.2, pred[128]{0:T(512)(128)(4,1)S(1)} %compare_and_fusion), kind=kOutput, calls=%fused_computation.21 | convolution fusion | flops 805830656 | bytes 12583040 | tf_op jit(solution)/shard_map/tij,ktj->kti/dot_general | solution.py:48
  213.5 2.1 fusion.6
  215.6 1.6 copy.36
  217.2 31.6 %reduce-scatter.8.cloned.1.call-done = f32[32,1024]{1,0:T(8,128)} async-done(((f32[32,8192]{1,0:T(8,128)}), f32[32,1024]{1,0:T(8,128)}) %reduce-scatter.8.cloned.1.call-update) | async-done | bytes 131088 | tf_op jit(solution)/shard_map/reduce_scatter | solution.py:52
  248.8 0.9 multiply_subtract_fusion
  249.7 0.3 fusion.42
  250.0 44.0 %psum.7 = f32[32,32]{1,0:T(8,128)S(1)} all-reduce(f32[32,32]{1,0:T(8,128)S(1)} %fusion.42), channel_id=1, replica_groups=mesh['row'=4,'col'=8] {'row','col'}, use_global_device_ids=true, to_apply=%region_5.7 | all-reduce | flops 1024 | bytes 8192 | tf_op jit(solution)/shard_map/psum | solution.py:62
  294.0 0.6 broadcast_multiply_fusion.1
  (33 shorter events, 0.4 us)
Async XLA Ops:
  7.2 101.8 %reduce-scatter.4.cloned.1.call-start = ((), (), s32[]{:S(2)}) async-start(), calls=%async_computation.3 | async-start | bytes 1179648 | tf_op jit(solution)/shard_map/reduce_scatter | solution.py:52
  7.2 5.7 %copy-start.3 = (s32[1,128]{1,0:T(1,128)S(1)}, s32[1,128]{1,0:T(1,128)}, u32[]{:S(2)}) copy-start(s32[1,128]{1,0:T(1,128)} %param.8) | copy-start | bytes 1540
  7.2 31.1 %copy-start.5 = (u32[32]{0:T(128)S(1)}, u32[32]{0:T(128)}, u32[]{:S(2)}) copy-start(u32[32]{0:T(128)} %constant.84) | copy-start | bytes 388
  7.3 32.4 %copy-start.1 = (f32[32,1024]{1,0:T(8,128)S(1)}, f32[32,1024]{1,0:T(8,128)}, u32[]{:S(2)}) copy-start(f32[32,1024]{1,0:T(8,128)} %param.6) | copy-start | bytes 393220
  7.3 34.0 %copy-start.4 = (s32[1,128]{1,0:T(1,128)S(1)}, s32[1,128]{1,0:T(1,128)}, u32[]{:S(2)}) copy-start(s32[1,128]{1,0:T(1,128)} %param.9) | copy-start | bytes 1540
  39.7 5.7 %collective-permute-start = (f32[32,1024]{1,0:T(8,128)S(1)}, f32[32,1024]{1,0:T(8,128)S(1)}, u32[]{:S(2)}, u32[]{:S(2)}) collective-permute-start(f32[32,1024]{1,0:T(8,128)S(1)} %get-tuple-element.8), channel_id=1, source_target_pairs={{0,8},{8,16},{16,24},{24,0},{1,9},{9,17},{17,25},{25,1},{2,10},{10... | collective-permute-start | bytes 393224 | tf_op jit(solution)/shard_map/ppermute | solution.py:21
  45.3 6.1 %collective-permute-start.1 = (f32[32,1024]{1,0:T(8,128)S(1)}, f32[32,1024]{1,0:T(8,128)S(1)}, u32[]{:S(2)}, u32[]{:S(2)}) collective-permute-start(f32[32,1024]{1,0:T(8,128)S(1)} %collective-permute-done), channel_id=1, source_target_pairs={{0,8},{8,16},{16,24},{24,0},{1,9},{9,17},{17,25},{25,1},{2,10},{10... | collective-permute-start | bytes 393224 | tf_op jit(solution)/shard_map/ppermute | solution.py:21
  51.4 5.9 %collective-permute-start.2 = (f32[32,1024]{1,0:T(8,128)S(1)}, f32[32,1024]{1,0:T(8,128)S(1)}, u32[]{:S(2)}, u32[]{:S(2)}) collective-permute-start(f32[32,1024]{1,0:T(8,128)S(1)} %collective-permute-done.1), channel_id=1, source_target_pairs={{0,8},{8,16},{16,24},{24,0},{1,9},{9,17},{17,25},{25,1},{2,10},{10... | collective-permute-start | bytes 393224 | tf_op jit(solution)/shard_map/ppermute | solution.py:21
  77.3 101.9 %reduce-scatter.6.cloned.1.call-start = ((), (), s32[]{:S(2)}) async-start(), calls=%async_computation.4 | async-start | bytes 1179648 | tf_op jit(solution)/shard_map/reduce_scatter | solution.py:52
  109.9 6.2 %collective-permute-start.3 = (f32[32,1024]{1,0:T(8,128)S(1)}, f32[32,1024]{1,0:T(8,128)S(1)}, u32[]{:S(2)}, u32[]{:S(2)}) collective-permute-start(f32[32,1024]{1,0:T(8,128)S(1)} %get-tuple-element.6), channel_id=1, source_target_pairs={{0,8},{8,16},{16,24},{24,0},{1,9},{9,17},{17,25},{25,1},{2,10},{10... | collective-permute-start | bytes 393224 | tf_op jit(solution)/shard_map/ppermute | solution.py:21
  116.2 5.3 %collective-permute-start.4 = (f32[32,1024]{1,0:T(8,128)S(1)}, f32[32,1024]{1,0:T(8,128)S(1)}, u32[]{:S(2)}, u32[]{:S(2)}) collective-permute-start(f32[32,1024]{1,0:T(8,128)S(1)} %collective-permute-done.3), channel_id=1, source_target_pairs={{0,8},{8,16},{16,24},{24,0},{1,9},{9,17},{17,25},{25,1},{2,10},{10... | collective-permute-start | bytes 393224 | tf_op jit(solution)/shard_map/ppermute | solution.py:21
  121.5 5.9 %collective-permute-start.5 = (f32[32,1024]{1,0:T(8,128)S(1)}, f32[32,1024]{1,0:T(8,128)S(1)}, u32[]{:S(2)}, u32[]{:S(2)}) collective-permute-start(f32[32,1024]{1,0:T(8,128)S(1)} %collective-permute-done.4), channel_id=1, source_target_pairs={{0,8},{8,16},{16,24},{24,0},{1,9},{9,17},{17,25},{25,1},{2,10},{10... | collective-permute-start | bytes 393224 | tf_op jit(solution)/shard_map/ppermute | solution.py:21
  147.4 101.4 %reduce-scatter.8.cloned.1.call-start = ((), (), s32[]{:S(2)}) async-start(), calls=%async_computation.5 | async-start | bytes 1179648 | tf_op jit(solution)/shard_map/reduce_scatter | solution.py:52
  180.2 6.0 %collective-permute-start.6 = (f32[32,1024]{1,0:T(8,128)S(1)}, f32[32,1024]{1,0:T(8,128)S(1)}, u32[]{:S(2)}, u32[]{:S(2)}) collective-permute-start(f32[32,1024]{1,0:T(8,128)S(1)} %get-tuple-element.4), channel_id=1, source_target_pairs={{0,8},{8,16},{16,24},{24,0},{1,9},{9,17},{17,25},{25,1},{2,10},{10... | collective-permute-start | bytes 393224 | tf_op jit(solution)/shard_map/ppermute | solution.py:21
  186.2 5.2 %collective-permute-start.7 = (f32[32,1024]{1,0:T(8,128)S(1)}, f32[32,1024]{1,0:T(8,128)S(1)}, u32[]{:S(2)}, u32[]{:S(2)}) collective-permute-start(f32[32,1024]{1,0:T(8,128)S(1)} %collective-permute-done.6), channel_id=1, source_target_pairs={{0,8},{8,16},{16,24},{24,0},{1,9},{9,17},{17,25},{25,1},{2,10},{10... | collective-permute-start | bytes 393224 | tf_op jit(solution)/shard_map/ppermute | solution.py:21
  191.4 5.8 %collective-permute-start.8 = (f32[32,1024]{1,0:T(8,128)S(1)}, f32[32,1024]{1,0:T(8,128)S(1)}, u32[]{:S(2)}, u32[]{:S(2)}) collective-permute-start(f32[32,1024]{1,0:T(8,128)S(1)} %collective-permute-done.7), channel_id=1, source_target_pairs={{0,8},{8,16},{16,24},{24,0},{1,9},{9,17},{17,25},{25,1},{2,10},{10... | collective-permute-start | bytes 393224 | tf_op jit(solution)/shard_map/ppermute | solution.py:21
  215.6 33.2 %copy-start.2 = (f32[32,1024]{1,0:T(8,128)S(1)}, f32[32,1024]{1,0:T(8,128)}, u32[]{:S(2)}) copy-start(f32[32,1024]{1,0:T(8,128)} %reduce-scatter.4.cloned.1.call-done) | copy-start | bytes 393220
  249.7 44.9 %copy-start = (f32[32,1024]{1,0:T(8,128)}, f32[32,1024]{1,0:T(8,128)S(1)}, u32[]{:S(2)}) copy-start(f32[32,1024]{1,0:T(8,128)S(1)} %multiply_subtract_fusion) | copy-start | bytes 393220
Sparse Core Ops, SparseCore 0:
  77.5 31.4 reduce-scatter.3
  147.5 31.6 reduce-scatter.5
  217.4 31.4 reduce-scatter.7
